TPU v7x, 32 devices: a whole 2x2x4 slice. The times are simulated.
32 devices in a mesh: section: 4 (over x, core), row: 4 (over z), col: 2 (over y).
Axes of the slice: x: 2, y: 2, z: 4, core: 2. Of those that a mesh axis runs over, the one named last changes fastest.
Arguments:
- latents: bfloat16 [2, 1280, 4, 128], P(None, 'col', 'row'), may hold values from -6 to 6
- timesteps: int32 [2], replicated, may hold values from 0 to 999
- weights: bfloat16 [4, 1280, 1280], P('section', 'row', 'col'), may hold values from -0.15625 to 0.15625
- taps: float32 [4, 3, 1280], P('section'), may hold values from -3 to 3
- time_table: bfloat16 [4, 1000, 1280], P('section'), may hold values from -5 to 5
- dilations: int32 [4], P('section'), may hold values from 1 to 4
Outputs:
- acts: bfloat16 [4, 2, 1280, 4, 128], P('section', None, 'col', 'row')
All inputs are finite; a program needn't handle non-finite values.
Results may differ from a plain program's by a relative error of at most 0.03.
Values may be sent and summed in bfloat16 or wider, within the bound.
A program may use at most 64 MiB of HBM per device.

v0:
```python
import jax
import jax.numpy as jnp
from jax import lax
from jax.sharding import PartitionSpec as P

DMAX = 4


def shifted(value, axis, steps):
    count = lax.axis_size(axis)
    first, last = (max(0, -steps), min(count, count - steps))
    return lax.ppermute(value, axis, [(source, source + steps) for source in range(first, last)])


def from_partner(block, axis, distance):
    count = lax.axis_size(axis)
    route = []
    for low in range(count):
        high = low | 1 << distance
        if high != low and high < count:
            route += [(low, high), (high, low)]
    return lax.ppermute(block, axis, route)


def activate(current, tap_rows, embedding, dilation, frame_count):
    widened = current.astype(jnp.float32)
    padded = jnp.pad(widened, ((0, 0), (0, 0), (DMAX, DMAX)))
    earlier = lax.dynamic_slice_in_dim(padded, DMAX - dilation, frame_count, 2)
    later_frames = lax.dynamic_slice_in_dim(padded, DMAX + dilation, frame_count, 2)
    summed = (
        tap_rows[0][:, None, None] * earlier
        + tap_rows[1][:, None, None] * widened
        + tap_rows[2][:, None, None] * later_frames
        + embedding[:, None, None]
    )
    return jax.nn.silu(summed).astype(jnp.bfloat16)


def per_device(latents, timesteps, weights, taps, time_table, dilations):
    section_count = lax.axis_size("section")
    section_id = lax.axis_index("section")
    col_index = lax.axis_index("col")
    micro_count = latents.shape[0]
    local_channels = latents.shape[1]
    frame_count = latents.shape[3]
    midpoint = section_count // 2
    bit_total = section_count.bit_length() - 1
    matrix_cols = lax.all_gather(weights[0], "row", axis=0, tiled=True)
    tap_all = taps[0]
    time_rows = time_table[0]
    dilation = dilations[0]

    def advance(tick_id, state_tuple, with_skip):
        incoming, kept, skip_store = state_tuple
        micro_id = tick_id - section_id
        active = (micro_id >= 0) & (micro_id < micro_count)
        slot_id = jnp.clip(micro_id, 0, micro_count - 1)
        entering = lax.dynamic_index_in_dim(latents, slot_id, 0, keepdims=False)
        current = jnp.where(section_id == 0, entering, incoming)
        step_id = lax.dynamic_index_in_dim(timesteps, slot_id, 0, keepdims=False)
        embedding = lax.dynamic_index_in_dim(time_rows, step_id, 0, keepdims=False).astype(
            jnp.float32
        )
        tap_mine = lax.dynamic_slice_in_dim(tap_all, col_index * local_channels, local_channels, 1)
        embed_mine = lax.dynamic_slice_in_dim(
            embedding, col_index * local_channels, local_channels, 0
        )
        activated = lax.all_gather(
            activate(current, tap_mine, embed_mine, dilation, frame_count),
            "col",
            axis=0,
            tiled=True,
        )
        mixed = lax.dot_general(
            matrix_cols,
            activated.reshape(activated.shape[0], -1),
            (((0,), (0,)), ((), ())),
            preferred_element_type=jnp.float32,
        ).reshape(current.shape)
        stored_skip = lax.dynamic_index_in_dim(skip_store, slot_id, 0, keepdims=False).astype(
            jnp.float32
        )
        skip_term = jnp.where(section_id >= midpoint, stored_skip, 0.0)
        result = (current.astype(jnp.float32) + mixed + skip_term).astype(jnp.bfloat16)
        previous = lax.dynamic_index_in_dim(kept, slot_id, 0, keepdims=False)
        kept = lax.dynamic_update_index_in_dim(
            kept, jnp.where(active, result, previous), slot_id, 0
        )
        incoming = shifted(result, "section", 1)
        if with_skip:
            mirrored = result
            bit_order = list(range(bit_total))
            for bit_number in bit_order:
                mirrored = from_partner(mirrored, "section", bit_number)
            source_micro = tick_id - (section_count - 1 - section_id)
            usable = (section_id >= midpoint) & (source_micro >= 0) & (source_micro < micro_count)
            source_slot = jnp.clip(source_micro, 0, micro_count - 1)
            held = lax.dynamic_index_in_dim(skip_store, source_slot, 0, keepdims=False)
            skip_store = lax.dynamic_update_index_in_dim(
                skip_store, jnp.where(usable, mirrored, held), source_slot, 0
            )
        return (incoming, kept, skip_store)

    blank = jnp.zeros(latents.shape[1:], jnp.bfloat16)
    initial = (
        blank,
        jnp.zeros(latents.shape, jnp.bfloat16),
        jnp.zeros(latents.shape, jnp.bfloat16),
    )
    first_end = micro_count + midpoint - 1
    state_tuple = lax.fori_loop(
        0, first_end, lambda tick_id, carried: advance(tick_id, carried, True), initial
    )
    state_tuple = lax.fori_loop(
        first_end,
        micro_count + section_count - 1,
        lambda tick_id, carried: advance(tick_id, carried, False),
        state_tuple,
    )
    return state_tuple[1][None]


def solution(mesh):
    in_specs = (
        P(None, "col", "row", None),
        P(),
        P("section", "row", "col"),
        P("section", None, None),
        P("section", None, None),
        P("section"),
    )
    out_specs = P("section", None, "col", "row", None)
    return jax.shard_map(
        per_device, mesh=mesh, in_specs=in_specs, out_specs=out_specs, check_vma=False
    )
```

profile of v0, /device:TPU:1, one launch (start us, length us, event | category | flops | bytes accessed | tf_op | source)
XLA Modules:
  0.0 153.2 jit_solution(2454798220183565018)
XLA Ops:
  8.0 1.2 copy.7
  9.2 40.0 %all-gather.3.cloned.1.call-done = bf16[1,1280,640]{2,1,0:T(8,128)(2,1)} async-done(((bf16[1,320,640]{2,1,0:T(8,128)(2,1)}), bf16[1,1280,640]{2,1,0:T(8,128)(2,1)}) %all-gather.3.cloned.1.call-update) | async-done | bytes 1638416 | tf_op jit(solution)/shard_map/all_gather | solution.py:48
  49.2 61.1 %while.38 = (s32[]{:T(128)}, bf16[640,1,128]{0,2,1:T(8,128)(2,1)S(1)}, bf16[2,640,1,128]{1,3,2,0:T(8,128)(2,1)S(1)}, bf16[2,640,1,128]{1,3,2,0:T(8,128)(2,1)S(1)...) while((s32[]{:T(128)}, ...), condition=%wide.region_1.2_spmd, body=%wide.region_0.1_spmd.sunk | while | flops 211354256 | bytes 14284052 | solution.py:111
  52.9 5.7 %all_gather.28 = bf16[1280,1,128]{0,2,1:T(8,128)(2,1)S(1)} all-gather(bf16[640,1,128]{0,2,1:T(8,128)(2,1)S(1)} %multiply_convert_fusion.4), channel_id=1, replica_groups=mesh['section'=4,'row'=4,'col'=2] {'col'}, dimensions={0}, use_global_device_ids=true | all-gather | bytes 491520 | tf_op jit(solution)/shard_map/while/body/eval_jaxpr/all_gather | solution.py:68
  58.6 1.1 bitcast_dynamic-update-slice_fusion.6
  59.7 1.6 %collective-permute-start.1 = (bf16[640,1,128]{0,2,1:T(8,128)(2,1)}, bf16[640,1,128]{0,2,1:T(8,128)(2,1)S(1)}, u32[]{:S(2)}, u32[]{:S(2)}) collective-permute-start(bf16[640,1,128]{0,2,1:T(8,128)(2,1)} %get-tuple-element.1072), channel_id=1, source_target_pairs={{0,8},{8,0},{16,24},{24,16},{1,9},{9,1},{17,25},{25,17},{2,10},{10... | collective-permute-start | bytes 491528 | tf_op jit(solution)/shard_map/while/body/eval_jaxpr/ppermute | solution.py:22
  61.3 1.2 collective-permute-done.1
  62.5 1.2 collective-permute-start.2
  63.7 2.7 %collective-permute-start = (bf16[640,1,128]{0,2,1:T(8,128)(2,1)}, bf16[640,1,128]{0,2,1:T(8,128)(2,1)S(1)}, u32[]{:S(2)}, u32[]{:S(2)}) collective-permute-start(bf16[640,1,128]{0,2,1:T(8,128)(2,1)} %get-tuple-element.1072), channel_id=1, source_target_pairs={{0,8},{8,16},{16,24},{1,9},{9,17},{17,25},{2,10},{10,18},{18,26},{... | collective-permute-start | bytes 491528 | tf_op jit(solution)/shard_map/while/body/eval_jaxpr/ppermute | solution.py:12
  66.5 1.5 collective-permute-done.2
  68.0 1.6 %collective-permute-done = bf16[640,1,128]{0,2,1:T(8,128)(2,1)S(1)} collective-permute-done((bf16[640,1,128]{0,2,1:T(8,128)(2,1)}, bf16[640,1,128]{0,2,1:T(8,128)(2,1)S(1)}, u32[]{:S(2)}, u32[]{:S(2)}) %collective-permute-start) | collective-permute-done | bytes 163872 | tf_op jit(solution)/shard_map/while/body/eval_jaxpr/ppermute | solution.py:12
  73.2 6.8 %all_gather.28 = bf16[1280,1,128]{0,2,1:T(8,128)(2,1)S(1)} all-gather(bf16[640,1,128]{0,2,1:T(8,128)(2,1)S(1)} %multiply_convert_fusion.4), channel_id=1, replica_groups=mesh['section'=4,'row'=4,'col'=2] {'col'}, dimensions={0}, use_global_device_ids=true | all-gather | bytes 491520 | tf_op jit(solution)/shard_map/while/body/eval_jaxpr/all_gather | solution.py:68
  80.0 1.1 bitcast_dynamic-update-slice_fusion.6
  81.6 1.2 collective-permute-done.1
  82.9 1.2 collective-permute-start.2
  84.1 2.7 %collective-permute-start = (bf16[640,1,128]{0,2,1:T(8,128)(2,1)}, bf16[640,1,128]{0,2,1:T(8,128)(2,1)S(1)}, u32[]{:S(2)}, u32[]{:S(2)}) collective-permute-start(bf16[640,1,128]{0,2,1:T(8,128)(2,1)} %get-tuple-element.1072), channel_id=1, source_target_pairs={{0,8},{8,16},{16,24},{1,9},{9,17},{17,25},{2,10},{10,18},{18,26},{... | collective-permute-start | bytes 491528 | tf_op jit(solution)/shard_map/while/body/eval_jaxpr/ppermute | solution.py:12
  86.8 1.5 collective-permute-done.2
  88.4 1.6 %collective-permute-done = bf16[640,1,128]{0,2,1:T(8,128)(2,1)S(1)} collective-permute-done((bf16[640,1,128]{0,2,1:T(8,128)(2,1)}, bf16[640,1,128]{0,2,1:T(8,128)(2,1)S(1)}, u32[]{:S(2)}, u32[]{:S(2)}) %collective-permute-start) | collective-permute-done | bytes 163872 | tf_op jit(solution)/shard_map/while/body/eval_jaxpr/ppermute | solution.py:12
  93.6 6.8 %all_gather.28 = bf16[1280,1,128]{0,2,1:T(8,128)(2,1)S(1)} all-gather(bf16[640,1,128]{0,2,1:T(8,128)(2,1)S(1)} %multiply_convert_fusion.4), channel_id=1, replica_groups=mesh['section'=4,'row'=4,'col'=2] {'col'}, dimensions={0}, use_global_device_ids=true | all-gather | bytes 491520 | tf_op jit(solution)/shard_map/while/body/eval_jaxpr/all_gather | solution.py:68
  102.0 1.2 collective-permute-done.1
  103.2 1.2 collective-permute-start.2
  104.4 2.7 %collective-permute-start = (bf16[640,1,128]{0,2,1:T(8,128)(2,1)}, bf16[640,1,128]{0,2,1:T(8,128)(2,1)S(1)}, u32[]{:S(2)}, u32[]{:S(2)}) collective-permute-start(bf16[640,1,128]{0,2,1:T(8,128)(2,1)} %get-tuple-element.1072), channel_id=1, source_target_pairs={{0,8},{8,16},{16,24},{1,9},{9,17},{17,25},{2,10},{10,18},{18,26},{... | collective-permute-start | bytes 491528 | tf_op jit(solution)/shard_map/while/body/eval_jaxpr/ppermute | solution.py:12
  107.2 1.5 collective-permute-done.2
  108.7 1.6 %collective-permute-done = bf16[640,1,128]{0,2,1:T(8,128)(2,1)S(1)} collective-permute-done((bf16[640,1,128]{0,2,1:T(8,128)(2,1)}, bf16[640,1,128]{0,2,1:T(8,128)(2,1)S(1)}, u32[]{:S(2)}, u32[]{:S(2)}) %collective-permute-start) | collective-permute-done | bytes 163872 | tf_op jit(solution)/shard_map/while/body/eval_jaxpr/ppermute | solution.py:12
  110.3 35.1 %while.39 = (s32[]{:T(128)}, bf16[640,1,128]{0,2,1:T(8,128)(2,1)S(1)}, bf16[2,640,1,128]{1,3,2,0:T(8,128)(2,1)S(1)}, pred[]{:T(512)}, s32[]{:T(128)}, /*index=5*...) while((s32[]{:T(128)}, ...), condition=%wide.region_3.4_spmd, body=%wide.region_2.3_spmd.sunk | while | flops 211272336 | bytes 12153995 | solution.py:114
  113.9 6.8 %all_gather.29 = bf16[1280,1,128]{0,2,1:T(8,128)(2,1)S(1)} all-gather(bf16[640,1,128]{0,2,1:T(8,128)(2,1)S(1)} %multiply_convert_fusion.5), channel_id=1, replica_groups=mesh['section'=4,'row'=4,'col'=2] {'col'}, dimensions={0}, use_global_device_ids=true | all-gather | bytes 491520 | tf_op jit(solution)/shard_map/while/body/eval_jaxpr/all_gather | solution.py:68
  121.8 3.5 %collective-permute-start.3 = (bf16[640,1,128]{0,2,1:T(8,128)(2,1)}, bf16[640,1,128]{0,2,1:T(8,128)(2,1)S(1)}, u32[]{:S(2)}, u32[]{:S(2)}) collective-permute-start(bf16[640,1,128]{0,2,1:T(8,128)(2,1)} %get-tuple-element.1093), channel_id=1, source_target_pairs={{0,8},{8,16},{16,24},{1,9},{9,17},{17,25},{2,10},{10,18},{18,26},{... | collective-permute-start | bytes 491528 | tf_op jit(solution)/shard_map/while/body/eval_jaxpr/ppermute | solution.py:12
  125.3 2.6 %collective-permute-done.3 = bf16[640,1,128]{0,2,1:T(8,128)(2,1)S(1)} collective-permute-done((bf16[640,1,128]{0,2,1:T(8,128)(2,1)}, bf16[640,1,128]{0,2,1:T(8,128)(2,1)S(1)}, u32[]{:S(2)}, u32[]{:S(2)}) %collective-permute-start.3) | collective-permute-done | bytes 163872 | tf_op jit(solution)/shard_map/while/body/eval_jaxpr/ppermute | solution.py:12
  131.5 4.8 %all_gather.29 = bf16[1280,1,128]{0,2,1:T(8,128)(2,1)S(1)} all-gather(bf16[640,1,128]{0,2,1:T(8,128)(2,1)S(1)} %multiply_convert_fusion.5), channel_id=1, replica_groups=mesh['section'=4,'row'=4,'col'=2] {'col'}, dimensions={0}, use_global_device_ids=true | all-gather | bytes 491520 | tf_op jit(solution)/shard_map/while/body/eval_jaxpr/all_gather | solution.py:68
  136.4 1.1 bitcast_dynamic-update-slice_fusion.8
  137.5 5.4 %collective-permute-start.3 = (bf16[640,1,128]{0,2,1:T(8,128)(2,1)}, bf16[640,1,128]{0,2,1:T(8,128)(2,1)S(1)}, u32[]{:S(2)}, u32[]{:S(2)}) collective-permute-start(bf16[640,1,128]{0,2,1:T(8,128)(2,1)} %get-tuple-element.1093), channel_id=1, source_target_pairs={{0,8},{8,16},{16,24},{1,9},{9,17},{17,25},{2,10},{10,18},{18,26},{... | collective-permute-start | bytes 491528 | tf_op jit(solution)/shard_map/while/body/eval_jaxpr/ppermute | solution.py:12
  142.9 2.6 %collective-permute-done.3 = bf16[640,1,128]{0,2,1:T(8,128)(2,1)S(1)} collective-permute-done((bf16[640,1,128]{0,2,1:T(8,128)(2,1)}, bf16[640,1,128]{0,2,1:T(8,128)(2,1)S(1)}, u32[]{:S(2)}, u32[]{:S(2)}) %collective-permute-start.3) | collective-permute-done | bytes 163872 | tf_op jit(solution)/shard_map/while/body/eval_jaxpr/ppermute | solution.py:12
  (57 shorter events, 13.4 us)
Async XLA Ops:
  6.5 1.4 copy-start
  6.5 42.7 %copy-start.3 = (s32[2]{0:T(128)S(1)}, s32[2]{0:T(128)}, u32[]{:S(2)}) copy-start(s32[2]{0:T(128)} %param.11) | copy-start | bytes 28
  6.5 42.6 %all-gather.3.cloned.1.call-start = ((), (), s32[]{:S(2)}) async-start(), calls=%async_computation | async-start | bytes 2048000 | tf_op jit(solution)/shard_map/all_gather | solution.py:48
  49.3 9.3 %copy-start.1 = (bf16[1280,640]{1,0:T(8,128)(2,1)S(1)}, bf16[1280,640]{1,0:T(8,128)(2,1)}, u32[]{:S(2)}) copy-start(bf16[1280,640]{1,0:T(8,128)(2,1)} %get-tuple-element.1148) | copy-start | bytes 4915204 | tf_op jit(solution)/shard_map/while
  59.7 2.9 %collective-permute-start.1 = (bf16[640,1,128]{0,2,1:T(8,128)(2,1)}, bf16[640,1,128]{0,2,1:T(8,128)(2,1)S(1)}, u32[]{:S(2)}, u32[]{:S(2)}) collective-permute-start(bf16[640,1,128]{0,2,1:T(8,128)(2,1)} %get-tuple-element.1072), channel_id=1, source_target_pairs={{0,8},{8,0},{16,24},{24,16},{1,9},{9,1},{17,25},{25,17},{2,10},{10... | collective-permute-start | bytes 491528 | tf_op jit(solution)/shard_map/while/body/eval_jaxpr/ppermute | solution.py:22
  62.5 5.4 %collective-permute-start.2 = (bf16[640,1,128]{0,2,1:T(8,128)(2,1)S(1)}, bf16[640,1,128]{0,2,1:T(8,128)(2,1)S(1)}, u32[]{:S(2)}, u32[]{:S(2)}) collective-permute-start(bf16[640,1,128]{0,2,1:T(8,128)(2,1)S(1)} %collective-permute-done.1), channel_id=1, source_target_pairs={{0,16},{16,0},{8,24},{24,8},{1,17},{17,1},{9,25},{25,9},{2,18},{18... | collective-permute-start | bytes 491528 | tf_op jit(solution)/shard_map/while/body/eval_jaxpr/ppermute | solution.py:22
  63.7 5.9 %collective-permute-start = (bf16[640,1,128]{0,2,1:T(8,128)(2,1)}, bf16[640,1,128]{0,2,1:T(8,128)(2,1)S(1)}, u32[]{:S(2)}, u32[]{:S(2)}) collective-permute-start(bf16[640,1,128]{0,2,1:T(8,128)(2,1)} %get-tuple-element.1072), channel_id=1, source_target_pairs={{0,8},{8,16},{16,24},{1,9},{9,17},{17,25},{2,10},{10,18},{18,26},{... | collective-permute-start | bytes 491528 | tf_op jit(solution)/shard_map/while/body/eval_jaxpr/ppermute | solution.py:12
  69.6 10.4 %copy-start.1 = (bf16[1280,640]{1,0:T(8,128)(2,1)S(1)}, bf16[1280,640]{1,0:T(8,128)(2,1)}, u32[]{:S(2)}) copy-start(bf16[1280,640]{1,0:T(8,128)(2,1)} %get-tuple-element.1148) | copy-start | bytes 4915204 | tf_op jit(solution)/shard_map/while
  81.1 1.7 %collective-permute-start.1 = (bf16[640,1,128]{0,2,1:T(8,128)(2,1)}, bf16[640,1,128]{0,2,1:T(8,128)(2,1)S(1)}, u32[]{:S(2)}, u32[]{:S(2)}) collective-permute-start(bf16[640,1,128]{0,2,1:T(8,128)(2,1)} %get-tuple-element.1072), channel_id=1, source_target_pairs={{0,8},{8,0},{16,24},{24,16},{1,9},{9,1},{17,25},{25,17},{2,10},{10... | collective-permute-start | bytes 491528 | tf_op jit(solution)/shard_map/while/body/eval_jaxpr/ppermute | solution.py:22
  82.9 5.4 %collective-permute-start.2 = (bf16[640,1,128]{0,2,1:T(8,128)(2,1)S(1)}, bf16[640,1,128]{0,2,1:T(8,128)(2,1)S(1)}, u32[]{:S(2)}, u32[]{:S(2)}) collective-permute-start(bf16[640,1,128]{0,2,1:T(8,128)(2,1)S(1)} %collective-permute-done.1), channel_id=1, source_target_pairs={{0,16},{16,0},{8,24},{24,8},{1,17},{17,1},{9,25},{25,9},{2,18},{18... | collective-permute-start | bytes 491528 | tf_op jit(solution)/shard_map/while/body/eval_jaxpr/ppermute | solution.py:22
  84.1 5.9 %collective-permute-start = (bf16[640,1,128]{0,2,1:T(8,128)(2,1)}, bf16[640,1,128]{0,2,1:T(8,128)(2,1)S(1)}, u32[]{:S(2)}, u32[]{:S(2)}) collective-permute-start(bf16[640,1,128]{0,2,1:T(8,128)(2,1)} %get-tuple-element.1072), channel_id=1, source_target_pairs={{0,8},{8,16},{16,24},{1,9},{9,17},{17,25},{2,10},{10,18},{18,26},{... | collective-permute-start | bytes 491528 | tf_op jit(solution)/shard_map/while/body/eval_jaxpr/ppermute | solution.py:12
  90.0 10.4 %copy-start.1 = (bf16[1280,640]{1,0:T(8,128)(2,1)S(1)}, bf16[1280,640]{1,0:T(8,128)(2,1)}, u32[]{:S(2)}) copy-start(bf16[1280,640]{1,0:T(8,128)(2,1)} %get-tuple-element.1148) | copy-start | bytes 4915204 | tf_op jit(solution)/shard_map/while
  101.5 1.7 %collective-permute-start.1 = (bf16[640,1,128]{0,2,1:T(8,128)(2,1)}, bf16[640,1,128]{0,2,1:T(8,128)(2,1)S(1)}, u32[]{:S(2)}, u32[]{:S(2)}) collective-permute-start(bf16[640,1,128]{0,2,1:T(8,128)(2,1)} %get-tuple-element.1072), channel_id=1, source_target_pairs={{0,8},{8,0},{16,24},{24,16},{1,9},{9,1},{17,25},{25,17},{2,10},{10... | collective-permute-start | bytes 491528 | tf_op jit(solution)/shard_map/while/body/eval_jaxpr/ppermute | solution.py:22
  103.2 5.4 %collective-permute-start.2 = (bf16[640,1,128]{0,2,1:T(8,128)(2,1)S(1)}, bf16[640,1,128]{0,2,1:T(8,128)(2,1)S(1)}, u32[]{:S(2)}, u32[]{:S(2)}) collective-permute-start(bf16[640,1,128]{0,2,1:T(8,128)(2,1)S(1)} %collective-permute-done.1), channel_id=1, source_target_pairs={{0,16},{16,0},{8,24},{24,8},{1,17},{17,1},{9,25},{25,9},{2,18},{18... | collective-permute-start | bytes 491528 | tf_op jit(solution)/shard_map/while/body/eval_jaxpr/ppermute | solution.py:22
  104.4 5.9 %collective-permute-start = (bf16[640,1,128]{0,2,1:T(8,128)(2,1)}, bf16[640,1,128]{0,2,1:T(8,128)(2,1)S(1)}, u32[]{:S(2)}, u32[]{:S(2)}) collective-permute-start(bf16[640,1,128]{0,2,1:T(8,128)(2,1)} %get-tuple-element.1072), channel_id=1, source_target_pairs={{0,8},{8,16},{16,24},{1,9},{9,17},{17,25},{2,10},{10,18},{18,26},{... | collective-permute-start | bytes 491528 | tf_op jit(solution)/shard_map/while/body/eval_jaxpr/ppermute | solution.py:12
  110.3 10.4 %copy-start.2 = (bf16[1280,640]{1,0:T(8,128)(2,1)S(1)}, bf16[1280,640]{1,0:T(8,128)(2,1)}, u32[]{:S(2)}) copy-start(bf16[1280,640]{1,0:T(8,128)(2,1)} %get-tuple-element.1207) | copy-start | bytes 4915204 | tf_op jit(solution)/shard_map/while
  121.8 6.0 %collective-permute-start.3 = (bf16[640,1,128]{0,2,1:T(8,128)(2,1)}, bf16[640,1,128]{0,2,1:T(8,128)(2,1)S(1)}, u32[]{:S(2)}, u32[]{:S(2)}) collective-permute-start(bf16[640,1,128]{0,2,1:T(8,128)(2,1)} %get-tuple-element.1093), channel_id=1, source_target_pairs={{0,8},{8,16},{16,24},{1,9},{9,17},{17,25},{2,10},{10,18},{18,26},{... | collective-permute-start | bytes 491528 | tf_op jit(solution)/shard_map/while/body/eval_jaxpr/ppermute | solution.py:12
  127.9 8.5 %copy-start.2 = (bf16[1280,640]{1,0:T(8,128)(2,1)S(1)}, bf16[1280,640]{1,0:T(8,128)(2,1)}, u32[]{:S(2)}) copy-start(bf16[1280,640]{1,0:T(8,128)(2,1)} %get-tuple-element.1207) | copy-start | bytes 4915204 | tf_op jit(solution)/shard_map/while
  137.5 8.0 %collective-permute-start.3 = (bf16[640,1,128]{0,2,1:T(8,128)(2,1)}, bf16[640,1,128]{0,2,1:T(8,128)(2,1)S(1)}, u32[]{:S(2)}, u32[]{:S(2)}) collective-permute-start(bf16[640,1,128]{0,2,1:T(8,128)(2,1)} %get-tuple-element.1093), channel_id=1, source_target_pairs={{0,8},{8,16},{16,24},{1,9},{9,17},{17,25},{2,10},{10,18},{18,26},{... | collective-permute-start | bytes 491528 | tf_op jit(solution)/shard_map/while/body/eval_jaxpr/ppermute | solution.py:12
Sparse Core Ops, SparseCore 0:
  8.9 40.1 all-gather.2
where the time goes:
time: 154 us; the launch traced here: 153 us
  waiting for transfers between devices  58.7 us (38%)
  blocking collectives  30.9 us (20%)
  starting transfers between devices  23.2 us (15%)
  between operations  14.1 us (9%)
  loops' own time  10 us (6%)
  matrix products  5.6 us (4%)
  other arithmetic  5.39 us (4%)
  local copies, waits for them, and re-layouts  5.24 us (3%)
    all_gather x1, waiting for transfers between devices, per_device(): matrix_cols = lax.all_gather(weights[0], 'row', axis=0, tiled=True)  40 us
    all_gather x5, blocking collectives, advance(): lax.all_gather(activate(current, tap_mine, embed_mine, dilation, frame_co...  30.9 us
    ppermute x5, starting transfers between devices, shifted(): lax.ppermute(value, axis, [(source, source + steps) for source in range(f...  17 us
    ppermute x5, waiting for transfers between devices, shifted(): lax.ppermute(value, axis, [(source, source + steps) for source in range(f...  9.91 us
    ppermute x6, waiting for transfers between devices, from_partner(): return lax.ppermute(block, axis, route)  8.13 us
    ppermute x6, starting transfers between devices, from_partner(): return lax.ppermute(block, axis, route)  6.22 us
    another operation x1, loops' own time, per_device(): lax.fori_loop(0, first_end, lambda tick_id, carried: advance(tick_id, car...  6.05 us
    dot_general x5, matrix products, advance(): lax.dot_general(matrix_cols, activated.reshape(activated.shape[0], -1), (...  5.6 us
  transfers between devices with their start and end apart: 12, of which 12 were waited for; matrix products, arithmetic and copies ran while one was open for 1% of the time, Pallas kernels for 0%

commit v1 on v0

--- a/solution.py
+++ b/solution.py
@@ -45,7 +45,12 @@
     frame_count = latents.shape[3]
     midpoint = section_count // 2
     bit_total = section_count.bit_length() - 1
-    matrix_cols = lax.all_gather(weights[0], "row", axis=0, tiled=True)
+    ring = [weights[0]]
+    for hop in range(3):
+        ring.append(lax.ppermute(ring[-1], "row", [(dev, (dev + 1) % 4) for dev in range(4)]))
+    matrix_cols = jnp.roll(
+        jnp.concatenate(ring[::-1], axis=0), (lax.axis_index("row") + 1) * ring[0].shape[0], axis=0
+    )
     tap_all = taps[0]
     time_rows = time_table[0]
     dilation = dilations[0]

time: 154 us -> 136 us (0.88)
  between operations: 14.1 us -> 0.84 us
  waiting for transfers between devices: 58.7 us -> 49.3 us
  starting transfers between devices: 23.2 us -> 28.2 us
    all_gather x1 -> x0, waiting for transfers between devices: 40 us -> none  [per_device(): matrix_cols = lax.all_gather(weights[0], 'row', axis=0, tiled=True)]
    ppermute x0 -> x3, waiting for transfers between devices: none -> 31.7 us  [per_device(): lax.ppermute(ring[-1], 'row', [(dev, (dev + 1) % 4) for dev in range(4)])]
    ppermute x6, starting transfers between devices: 6.22 us -> 8.71 us  [from_partner(): return lax.ppermute(block, axis, route)]
    ppermute x0 -> x3, starting transfers between devices: none -> 2.13 us  [per_device(): lax.ppermute(ring[-1], 'row', [(dev, (dev + 1) % 4) for dev in range(4)])]
  transfers between devices with their start and end apart: 12 -> 14, of which waited for: 12 -> 14; matrix products, arithmetic and copies ran while one was open for 1% -> 1% of each run, Pallas kernels for 0% -> 0%
where the time goes in v1:
time: 136 us; the launch traced here: 135 us
  waiting for transfers between devices  49.3 us (36%)
  blocking collectives  29.7 us (22%)
  starting transfers between devices  28.2 us (21%)
  loops' own time  9.98 us (7%)
  local copies, waits for them, and re-layouts  6.04 us (4%)
  matrix products  5.62 us (4%)
  other arithmetic  5.39 us (4%)
    ppermute x3, waiting for transfers between devices, per_device(): lax.ppermute(ring[-1], 'row', [(dev, (dev + 1) % 4) for dev in range(4)])  31.7 us
    all_gather x5, blocking collectives, advance(): lax.all_gather(activate(current, tap_mine, embed_mine, dilation, frame_co...  29.7 us
    ppermute x5, starting transfers between devices, shifted(): lax.ppermute(value, axis, [(source, source + steps) for source in range(f...  17.4 us
    ppermute x5, waiting for transfers between devices, shifted(): lax.ppermute(value, axis, [(source, source + steps) for source in range(f...  9.5 us
    ppermute x6, starting transfers between devices, from_partner(): return lax.ppermute(block, axis, route)  8.71 us
    ppermute x6, waiting for transfers between devices, from_partner(): return lax.ppermute(block, axis, route)  8.13 us
    another operation x1, loops' own time, per_device(): lax.fori_loop(0, first_end, lambda tick_id, carried: advance(tick_id, car...  6.02 us
    dot_general x5, matrix products, advance(): lax.dot_general(matrix_cols, activated.reshape(activated.shape[0], -1), (...  5.62 us
  transfers between devices with their start and end apart: 14, of which 14 were waited for; matrix products, arithmetic and copies ran while one was open for 1% of the time, Pallas kernels for 0%

profile of v1, /device:TPU:1, one launch (start us, length us, event | category | flops | bytes accessed | tf_op | source)
XLA Modules:
  0.0 135.1 jit_solution(2101420674557445147)
XLA Ops:
  0.0 2.1 %collective-permute-start.4 = (bf16[320,640]{1,0:T(8,128)(2,1)}, bf16[320,640]{1,0:T(8,128)(2,1)S(1)}, u32[]{:S(2)}, u32[]{:S(2)}) collective-permute-start(bf16[320,640]{1,0:T(8,128)(2,1)} %bitcast.104), channel_id=1, source_target_pairs={{0,2},{2,4},{4,6},{6,0},{1,3},{3,5},{5,7},{7,1},{8,10},{10,12},{12... | collective-permute-start | bytes 1228808 | tf_op jit(solution)/shard_map/ppermute | solution.py:50
  2.1 11.5 %collective-permute-done.4 = bf16[320,640]{1,0:T(8,128)(2,1)S(1)} collective-permute-done((bf16[320,640]{1,0:T(8,128)(2,1)}, bf16[320,640]{1,0:T(8,128)(2,1)S(1)}, u32[]{:S(2)}, u32[]{:S(2)}) %collective-permute-start.4) | collective-permute-done | bytes 409632 | tf_op jit(solution)/shard_map/ppermute | solution.py:50
  13.6 11.5 %collective-permute-done.5 = bf16[320,640]{1,0:T(8,128)(2,1)S(1)} collective-permute-done((bf16[320,640]{1,0:T(8,128)(2,1)S(1)}, bf16[320,640]{1,0:T(8,128)(2,1)S(1)}, u32[]{:S(2)}, u32[]{:S(2)}) %collective-permute-start.5) | collective-permute-done | bytes 409632 | tf_op jit(solution)/shard_map/ppermute | solution.py:50
  25.8 1.2 copy.7
  27.0 8.7 %collective-permute-done.6 = bf16[320,640]{1,0:T(8,128)(2,1)S(1)} collective-permute-done((bf16[320,640]{1,0:T(8,128)(2,1)S(1)}, bf16[320,640]{1,0:T(8,128)(2,1)S(1)}, u32[]{:S(2)}, u32[]{:S(2)}) %collective-permute-start.6) | collective-permute-done | bytes 409632 | tf_op jit(solution)/shard_map/ppermute | solution.py:50
  36.7 62.4 %while.38 = (s32[]{:T(128)}, bf16[640,1,128]{0,2,1:T(8,128)(2,1)S(1)}, bf16[2,640,1,128]{1,3,2,0:T(8,128)(2,1)S(1)}, bf16[2,640,1,128]{1,3,2,0:T(8,128)(2,1)S(1)...) while((s32[]{:T(128)}, ...), condition=%wide.region_1.2_spmd, body=%wide.region_0.1_spmd.sunk | while | flops 211354256 | bytes 7730424 | solution.py:116
  40.3 4.8 %all_gather.24 = bf16[1280,1,128]{0,2,1:T(8,128)(2,1)S(1)} all-gather(bf16[640,1,128]{0,2,1:T(8,128)(2,1)S(1)} %multiply_convert_fusion.4), channel_id=1, replica_groups=mesh['section'=4,'row'=4,'col'=2] {'col'}, dimensions={0}, use_global_device_ids=true | all-gather | bytes 491520 | tf_op jit(solution)/shard_map/while/body/eval_jaxpr/all_gather | solution.py:73
  46.3 4.2 %collective-permute-start.1 = (bf16[640,1,128]{0,2,1:T(8,128)(2,1)}, bf16[640,1,128]{0,2,1:T(8,128)(2,1)S(1)}, u32[]{:S(2)}, u32[]{:S(2)}) collective-permute-start(bf16[640,1,128]{0,2,1:T(8,128)(2,1)} %get-tuple-element.1072), channel_id=1, source_target_pairs={{0,8},{8,0},{16,24},{24,16},{1,9},{9,1},{17,25},{25,17},{2,10},{10... | collective-permute-start | bytes 491528 | tf_op jit(solution)/shard_map/while/body/eval_jaxpr/ppermute | solution.py:22
  50.5 1.2 collective-permute-done.1
  52.6 3.1 %collective-permute-start = (bf16[640,1,128]{0,2,1:T(8,128)(2,1)}, bf16[640,1,128]{0,2,1:T(8,128)(2,1)S(1)}, u32[]{:S(2)}, u32[]{:S(2)}) collective-permute-start(bf16[640,1,128]{0,2,1:T(8,128)(2,1)} %get-tuple-element.1072), channel_id=1, source_target_pairs={{0,8},{8,16},{16,24},{1,9},{9,17},{17,25},{2,10},{10,18},{18,26},{... | collective-permute-start | bytes 491528 | tf_op jit(solution)/shard_map/while/body/eval_jaxpr/ppermute | solution.py:12
  55.7 1.5 %collective-permute-done.2 = bf16[640,1,128]{0,2,1:T(8,128)(2,1)S(1)} collective-permute-done((bf16[640,1,128]{0,2,1:T(8,128)(2,1)S(1)}, bf16[640,1,128]{0,2,1:T(8,128)(2,1)S(1)}, u32[]{:S(2)}, u32[]{:S(2)}) %collective-permute-start.2) | collective-permute-done | bytes 163872 | tf_op jit(solution)/shard_map/while/body/eval_jaxpr/ppermute | solution.py:22
  57.3 1.2 collective-permute-done
  62.0 6.5 %all_gather.24 = bf16[1280,1,128]{0,2,1:T(8,128)(2,1)S(1)} all-gather(bf16[640,1,128]{0,2,1:T(8,128)(2,1)S(1)} %multiply_convert_fusion.4), channel_id=1, replica_groups=mesh['section'=4,'row'=4,'col'=2] {'col'}, dimensions={0}, use_global_device_ids=true | all-gather | bytes 491520 | tf_op jit(solution)/shard_map/while/body/eval_jaxpr/all_gather | solution.py:73
  70.5 1.2 collective-permute-done.1
  71.7 1.2 collective-permute-start.2
  72.9 2.7 %collective-permute-start = (bf16[640,1,128]{0,2,1:T(8,128)(2,1)}, bf16[640,1,128]{0,2,1:T(8,128)(2,1)S(1)}, u32[]{:S(2)}, u32[]{:S(2)}) collective-permute-start(bf16[640,1,128]{0,2,1:T(8,128)(2,1)} %get-tuple-element.1072), channel_id=1, source_target_pairs={{0,8},{8,16},{16,24},{1,9},{9,17},{17,25},{2,10},{10,18},{18,26},{... | collective-permute-start | bytes 491528 | tf_op jit(solution)/shard_map/while/body/eval_jaxpr/ppermute | solution.py:12
  75.7 1.5 %collective-permute-done.2 = bf16[640,1,128]{0,2,1:T(8,128)(2,1)S(1)} collective-permute-done((bf16[640,1,128]{0,2,1:T(8,128)(2,1)S(1)}, bf16[640,1,128]{0,2,1:T(8,128)(2,1)S(1)}, u32[]{:S(2)}, u32[]{:S(2)}) %collective-permute-start.2) | collective-permute-done | bytes 163872 | tf_op jit(solution)/shard_map/while/body/eval_jaxpr/ppermute | solution.py:22
  77.2 1.6 %collective-permute-done = bf16[640,1,128]{0,2,1:T(8,128)(2,1)S(1)} collective-permute-done((bf16[640,1,128]{0,2,1:T(8,128)(2,1)}, bf16[640,1,128]{0,2,1:T(8,128)(2,1)S(1)}, u32[]{:S(2)}, u32[]{:S(2)}) %collective-permute-start) | collective-permute-done | bytes 163872 | tf_op jit(solution)/shard_map/while/body/eval_jaxpr/ppermute | solution.py:12
  82.4 6.8 %all_gather.24 = bf16[1280,1,128]{0,2,1:T(8,128)(2,1)S(1)} all-gather(bf16[640,1,128]{0,2,1:T(8,128)(2,1)S(1)} %multiply_convert_fusion.4), channel_id=1, replica_groups=mesh['section'=4,'row'=4,'col'=2] {'col'}, dimensions={0}, use_global_device_ids=true | all-gather | bytes 491520 | tf_op jit(solution)/shard_map/while/body/eval_jaxpr/all_gather | solution.py:73
  89.2 1.1 bitcast_dynamic-update-slice_fusion.6
  90.8 1.2 collective-permute-done.1
  92.0 1.2 collective-permute-start.2
  93.2 2.7 %collective-permute-start = (bf16[640,1,128]{0,2,1:T(8,128)(2,1)}, bf16[640,1,128]{0,2,1:T(8,128)(2,1)S(1)}, u32[]{:S(2)}, u32[]{:S(2)}) collective-permute-start(bf16[640,1,128]{0,2,1:T(8,128)(2,1)} %get-tuple-element.1072), channel_id=1, source_target_pairs={{0,8},{8,16},{16,24},{1,9},{9,17},{17,25},{2,10},{10,18},{18,26},{... | collective-permute-start | bytes 491528 | tf_op jit(solution)/shard_map/while/body/eval_jaxpr/ppermute | solution.py:12
  96.0 1.5 %collective-permute-done.2 = bf16[640,1,128]{0,2,1:T(8,128)(2,1)S(1)} collective-permute-done((bf16[640,1,128]{0,2,1:T(8,128)(2,1)S(1)}, bf16[640,1,128]{0,2,1:T(8,128)(2,1)S(1)}, u32[]{:S(2)}, u32[]{:S(2)}) %collective-permute-start.2) | collective-permute-done | bytes 163872 | tf_op jit(solution)/shard_map/while/body/eval_jaxpr/ppermute | solution.py:22
  97.5 1.6 %collective-permute-done = bf16[640,1,128]{0,2,1:T(8,128)(2,1)S(1)} collective-permute-done((bf16[640,1,128]{0,2,1:T(8,128)(2,1)}, bf16[640,1,128]{0,2,1:T(8,128)(2,1)S(1)}, u32[]{:S(2)}, u32[]{:S(2)}) %collective-permute-start) | collective-permute-done | bytes 163872 | tf_op jit(solution)/shard_map/while/body/eval_jaxpr/ppermute | solution.py:12
  99.1 35.1 %while.39 = (s32[]{:T(128)}, bf16[640,1,128]{0,2,1:T(8,128)(2,1)S(1)}, bf16[2,640,1,128]{1,3,2,0:T(8,128)(2,1)S(1)}, pred[]{:T(512)}, s32[]{:T(128)}, /*index=5*...) while((s32[]{:T(128)}, ...), condition=%wide.region_3.4_spmd, body=%wide.region_2.3_spmd.sunk | while | flops 211272336 | bytes 5600367 | solution.py:119
  102.7 6.8 %all_gather.25 = bf16[1280,1,128]{0,2,1:T(8,128)(2,1)S(1)} all-gather(bf16[640,1,128]{0,2,1:T(8,128)(2,1)S(1)} %multiply_convert_fusion.5), channel_id=1, replica_groups=mesh['section'=4,'row'=4,'col'=2] {'col'}, dimensions={0}, use_global_device_ids=true | all-gather | bytes 491520 | tf_op jit(solution)/shard_map/while/body/eval_jaxpr/all_gather | solution.py:73
  110.6 3.5 %collective-permute-start.3 = (bf16[640,1,128]{0,2,1:T(8,128)(2,1)}, bf16[640,1,128]{0,2,1:T(8,128)(2,1)S(1)}, u32[]{:S(2)}, u32[]{:S(2)}) collective-permute-start(bf16[640,1,128]{0,2,1:T(8,128)(2,1)} %get-tuple-element.1093), channel_id=1, source_target_pairs={{0,8},{8,16},{16,24},{1,9},{9,17},{17,25},{2,10},{10,18},{18,26},{... | collective-permute-start | bytes 491528 | tf_op jit(solution)/shard_map/while/body/eval_jaxpr/ppermute | solution.py:12
  114.1 2.6 %collective-permute-done.3 = bf16[640,1,128]{0,2,1:T(8,128)(2,1)S(1)} collective-permute-done((bf16[640,1,128]{0,2,1:T(8,128)(2,1)}, bf16[640,1,128]{0,2,1:T(8,128)(2,1)S(1)}, u32[]{:S(2)}, u32[]{:S(2)}) %collective-permute-start.3) | collective-permute-done | bytes 163872 | tf_op jit(solution)/shard_map/while/body/eval_jaxpr/ppermute | solution.py:12
  120.2 4.8 %all_gather.25 = bf16[1280,1,128]{0,2,1:T(8,128)(2,1)S(1)} all-gather(bf16[640,1,128]{0,2,1:T(8,128)(2,1)S(1)} %multiply_convert_fusion.5), channel_id=1, replica_groups=mesh['section'=4,'row'=4,'col'=2] {'col'}, dimensions={0}, use_global_device_ids=true | all-gather | bytes 491520 | tf_op jit(solution)/shard_map/while/body/eval_jaxpr/all_gather | solution.py:73
  126.2 5.4 %collective-permute-start.3 = (bf16[640,1,128]{0,2,1:T(8,128)(2,1)}, bf16[640,1,128]{0,2,1:T(8,128)(2,1)S(1)}, u32[]{:S(2)}, u32[]{:S(2)}) collective-permute-start(bf16[640,1,128]{0,2,1:T(8,128)(2,1)} %get-tuple-element.1093), channel_id=1, source_target_pairs={{0,8},{8,16},{16,24},{1,9},{9,17},{17,25},{2,10},{10,18},{18,26},{... | collective-permute-start | bytes 491528 | tf_op jit(solution)/shard_map/while/body/eval_jaxpr/ppermute | solution.py:12
  131.7 2.6 %collective-permute-done.3 = bf16[640,1,128]{0,2,1:T(8,128)(2,1)S(1)} collective-permute-done((bf16[640,1,128]{0,2,1:T(8,128)(2,1)}, bf16[640,1,128]{0,2,1:T(8,128)(2,1)S(1)}, u32[]{:S(2)}, u32[]{:S(2)}) %collective-permute-start.3) | collective-permute-done | bytes 163872 | tf_op jit(solution)/shard_map/while/body/eval_jaxpr/ppermute | solution.py:12
  (61 shorter events, 16.9 us)
Async XLA Ops:
  0.0 25.8 %copy-start = (f32[1,3,1280]{2,0,1:T(1,128)S(1)}, f32[1,3,1280]{2,0,1:T(1,128)}, u32[]{:S(2)}) copy-start(f32[1,3,1280]{2,0,1:T(1,128)} %param.13) | copy-start | bytes 46084
  0.0 35.9 %copy-start.1 = (bf16[1,320,640]{2,1,0:T(8,128)(2,1)S(1)}, bf16[1,320,640]{2,1,0:T(8,128)(2,1)}, u32[]{:S(2)}) copy-start(bf16[1,320,640]{2,1,0:T(8,128)(2,1)} %param.12) | copy-start | bytes 1228804
  0.0 13.6 %collective-permute-start.4 = (bf16[320,640]{1,0:T(8,128)(2,1)}, bf16[320,640]{1,0:T(8,128)(2,1)S(1)}, u32[]{:S(2)}, u32[]{:S(2)}) collective-permute-start(bf16[320,640]{1,0:T(8,128)(2,1)} %bitcast.104), channel_id=1, source_target_pairs={{0,2},{2,4},{4,6},{6,0},{1,3},{3,5},{5,7},{7,1},{8,10},{10,12},{12... | collective-permute-start | bytes 1228808 | tf_op jit(solution)/shard_map/ppermute | solution.py:50
  13.6 11.5 %collective-permute-start.5 = (bf16[320,640]{1,0:T(8,128)(2,1)S(1)}, bf16[320,640]{1,0:T(8,128)(2,1)S(1)}, u32[]{:S(2)}, u32[]{:S(2)}) collective-permute-start(bf16[320,640]{1,0:T(8,128)(2,1)S(1)} %collective-permute-done.4), channel_id=1, source_target_pairs={{0,2},{2,4},{4,6},{6,0},{1,3},{3,5},{5,7},{7,1},{8,10},{10,12},{12... | collective-permute-start | bytes 1228808 | tf_op jit(solution)/shard_map/ppermute | solution.py:50
  25.1 10.6 %collective-permute-start.6 = (bf16[320,640]{1,0:T(8,128)(2,1)S(1)}, bf16[320,640]{1,0:T(8,128)(2,1)S(1)}, u32[]{:S(2)}, u32[]{:S(2)}) collective-permute-start(bf16[320,640]{1,0:T(8,128)(2,1)S(1)} %collective-permute-done.5), channel_id=1, source_target_pairs={{0,2},{2,4},{4,6},{6,0},{1,3},{3,5},{5,7},{7,1},{8,10},{10,12},{12... | collective-permute-start | bytes 1228808 | tf_op jit(solution)/shard_map/ppermute | solution.py:50
  36.0 0.7 copy-start.2
  46.3 5.5 %collective-permute-start.1 = (bf16[640,1,128]{0,2,1:T(8,128)(2,1)}, bf16[640,1,128]{0,2,1:T(8,128)(2,1)S(1)}, u32[]{:S(2)}, u32[]{:S(2)}) collective-permute-start(bf16[640,1,128]{0,2,1:T(8,128)(2,1)} %get-tuple-element.1072), channel_id=1, source_target_pairs={{0,8},{8,0},{16,24},{24,16},{1,9},{9,1},{17,25},{25,17},{2,10},{10... | collective-permute-start | bytes 491528 | tf_op jit(solution)/shard_map/while/body/eval_jaxpr/ppermute | solution.py:22
  51.8 5.4 %collective-permute-start.2 = (bf16[640,1,128]{0,2,1:T(8,128)(2,1)S(1)}, bf16[640,1,128]{0,2,1:T(8,128)(2,1)S(1)}, u32[]{:S(2)}, u32[]{:S(2)}) collective-permute-start(bf16[640,1,128]{0,2,1:T(8,128)(2,1)S(1)} %collective-permute-done.1), channel_id=1, source_target_pairs={{0,16},{16,0},{8,24},{24,8},{1,17},{17,1},{9,25},{25,9},{2,18},{18... | collective-permute-start | bytes 491528 | tf_op jit(solution)/shard_map/while/body/eval_jaxpr/ppermute | solution.py:22
  52.6 5.9 %collective-permute-start = (bf16[640,1,128]{0,2,1:T(8,128)(2,1)}, bf16[640,1,128]{0,2,1:T(8,128)(2,1)S(1)}, u32[]{:S(2)}, u32[]{:S(2)}) collective-permute-start(bf16[640,1,128]{0,2,1:T(8,128)(2,1)} %get-tuple-element.1072), channel_id=1, source_target_pairs={{0,8},{8,16},{16,24},{1,9},{9,17},{17,25},{2,10},{10,18},{18,26},{... | collective-permute-start | bytes 491528 | tf_op jit(solution)/shard_map/while/body/eval_jaxpr/ppermute | solution.py:12
  69.6 2.1 %collective-permute-start.1 = (bf16[640,1,128]{0,2,1:T(8,128)(2,1)}, bf16[640,1,128]{0,2,1:T(8,128)(2,1)S(1)}, u32[]{:S(2)}, u32[]{:S(2)}) collective-permute-start(bf16[640,1,128]{0,2,1:T(8,128)(2,1)} %get-tuple-element.1072), channel_id=1, source_target_pairs={{0,8},{8,0},{16,24},{24,16},{1,9},{9,1},{17,25},{25,17},{2,10},{10... | collective-permute-start | bytes 491528 | tf_op jit(solution)/shard_map/while/body/eval_jaxpr/ppermute | solution.py:22
  71.7 5.4 %collective-permute-start.2 = (bf16[640,1,128]{0,2,1:T(8,128)(2,1)S(1)}, bf16[640,1,128]{0,2,1:T(8,128)(2,1)S(1)}, u32[]{:S(2)}, u32[]{:S(2)}) collective-permute-start(bf16[640,1,128]{0,2,1:T(8,128)(2,1)S(1)} %collective-permute-done.1), channel_id=1, source_target_pairs={{0,16},{16,0},{8,24},{24,8},{1,17},{17,1},{9,25},{25,9},{2,18},{18... | collective-permute-start | bytes 491528 | tf_op jit(solution)/shard_map/while/body/eval_jaxpr/ppermute | solution.py:22
  72.9 5.9 %collective-permute-start = (bf16[640,1,128]{0,2,1:T(8,128)(2,1)}, bf16[640,1,128]{0,2,1:T(8,128)(2,1)S(1)}, u32[]{:S(2)}, u32[]{:S(2)}) collective-permute-start(bf16[640,1,128]{0,2,1:T(8,128)(2,1)} %get-tuple-element.1072), channel_id=1, source_target_pairs={{0,8},{8,16},{16,24},{1,9},{9,17},{17,25},{2,10},{10,18},{18,26},{... | collective-permute-start | bytes 491528 | tf_op jit(solution)/shard_map/while/body/eval_jaxpr/ppermute | solution.py:12
  90.3 1.7 %collective-permute-start.1 = (bf16[640,1,128]{0,2,1:T(8,128)(2,1)}, bf16[640,1,128]{0,2,1:T(8,128)(2,1)S(1)}, u32[]{:S(2)}, u32[]{:S(2)}) collective-permute-start(bf16[640,1,128]{0,2,1:T(8,128)(2,1)} %get-tuple-element.1072), channel_id=1, source_target_pairs={{0,8},{8,0},{16,24},{24,16},{1,9},{9,1},{17,25},{25,17},{2,10},{10... | collective-permute-start | bytes 491528 | tf_op jit(solution)/shard_map/while/body/eval_jaxpr/ppermute | solution.py:22
  92.0 5.4 %collective-permute-start.2 = (bf16[640,1,128]{0,2,1:T(8,128)(2,1)S(1)}, bf16[640,1,128]{0,2,1:T(8,128)(2,1)S(1)}, u32[]{:S(2)}, u32[]{:S(2)}) collective-permute-start(bf16[640,1,128]{0,2,1:T(8,128)(2,1)S(1)} %collective-permute-done.1), channel_id=1, source_target_pairs={{0,16},{16,0},{8,24},{24,8},{1,17},{17,1},{9,25},{25,9},{2,18},{18... | collective-permute-start | bytes 491528 | tf_op jit(solution)/shard_map/while/body/eval_jaxpr/ppermute | solution.py:22
  93.2 5.9 %collective-permute-start = (bf16[640,1,128]{0,2,1:T(8,128)(2,1)}, bf16[640,1,128]{0,2,1:T(8,128)(2,1)S(1)}, u32[]{:S(2)}, u32[]{:S(2)}) collective-permute-start(bf16[640,1,128]{0,2,1:T(8,128)(2,1)} %get-tuple-element.1072), channel_id=1, source_target_pairs={{0,8},{8,16},{16,24},{1,9},{9,17},{17,25},{2,10},{10,18},{18,26},{... | collective-permute-start | bytes 491528 | tf_op jit(solution)/shard_map/while/body/eval_jaxpr/ppermute | solution.py:12
  110.6 6.0 %collective-permute-start.3 = (bf16[640,1,128]{0,2,1:T(8,128)(2,1)}, bf16[640,1,128]{0,2,1:T(8,128)(2,1)S(1)}, u32[]{:S(2)}, u32[]{:S(2)}) collective-permute-start(bf16[640,1,128]{0,2,1:T(8,128)(2,1)} %get-tuple-element.1093), channel_id=1, source_target_pairs={{0,8},{8,16},{16,24},{1,9},{9,17},{17,25},{2,10},{10,18},{18,26},{... | collective-permute-start | bytes 491528 | tf_op jit(solution)/shard_map/while/body/eval_jaxpr/ppermute | solution.py:12
  126.2 8.0 %collective-permute-start.3 = (bf16[640,1,128]{0,2,1:T(8,128)(2,1)}, bf16[640,1,128]{0,2,1:T(8,128)(2,1)S(1)}, u32[]{:S(2)}, u32[]{:S(2)}) collective-permute-start(bf16[640,1,128]{0,2,1:T(8,128)(2,1)} %get-tuple-element.1093), channel_id=1, source_target_pairs={{0,8},{8,16},{16,24},{1,9},{9,17},{17,25},{2,10},{10,18},{18,26},{... | collective-permute-start | bytes 491528 | tf_op jit(solution)/shard_map/while/body/eval_jaxpr/ppermute | solution.py:12
